TPU v7x, 32 devices: a whole 2x2x4 slice. The times are simulated.
32 devices in a mesh: groups: 2 (over x), span: 16 (over z, y, core).
Axes of the slice: x: 2, y: 2, z: 4, core: 2. Of those that a mesh axis runs over, the one named last changes fastest.
Arguments:
- hidden_in: bfloat16 [16384, 2240], P(('groups', 'span')), parts along dimension 0, may hold values from -16 to 16
- noisy_latents: float32 [16384, 32], P(('groups', 'span')), parts along dimension 0, may hold values from -6 to 6
- span_ids: int32 [16384], P(('groups', 'span')), parts along dimension 0, may hold values from 0 to 31, as said below
- tile_map: int32 [16384], P('groups'), parts along dimension 0, may hold values from 0 to 8191, as said below
- qkv_weight: bfloat16 [2240, 3360], replicated, may hold values from -0.125 to 0.125
- out_weight: bfloat16 [1120, 2240], replicated, may hold values from -0.1875 to 0.1875
- norm_gain: float32 [2240], replicated, may hold values from 0.1 to 1.9
- velocity_weight: bfloat16 [2240, 32], replicated, may hold values from -0.125 to 0.125
- conv_first: bfloat16 [3, 3, 32, 256], replicated, may hold values from -0.375 to 0.375
- conv_second: bfloat16 [3, 3, 256, 256], replicated, may hold values from -0.125 to 0.125
Outputs:
- new_latents: float32 [16384, 32], P(('groups', 'span')), parts along dimension 0
- decoded: bfloat16 [256, 64, 256], P(('groups', 'span')), parts along dimension 0
There are 2 independent parts, one for each index of `groups`. A program takes and returns all parts, laid end to end along the dimension named above; an argument that names none is the same for every part. Nothing has to cross between parts.
Inputs may be any that keep to these rules, and one draw needn't show every extreme that they name: `span_ids`: never falling along the tokens; every span number occurs, each span holds 1 to 1024 tokens, and one span holds exactly 1024. `tile_map`: A permutation of the 8192 grid positions; the 512 tokens of each aligned block of tokens place exactly 32 tokens in each aligned block of 512 positions.
All inputs are finite; a program needn't handle non-finite values.
Results may differ from a plain program's by a relative error of at most 0.01.
Values may be sent and summed in bfloat16 or wider, within the bound.
A program may use at most 128 MiB of HBM per device.

v0:
```python
import jax
import jax.numpy as jnp
from jax import lax
from jax.sharding import PartitionSpec as P

HDIM = 32
C = 32
IW = 64


def padded_2(x, sides, width):
    for axis, dim in sides:
        devices, length = (lax.axis_size(axis), x.shape[dim])
        up = [(i, (i + 1) % devices) for i in range(devices - 1)]
        down = [(j, i) for i, j in up]
        last = lax.slice_in_dim(x, length - width, length, axis=dim)
        first = lax.slice_in_dim(x, 0, width, axis=dim)
        before = lax.ppermute(last, axis, up)
        after = lax.ppermute(first, axis, down)
        x = jnp.concatenate([before, x, after], axis=dim)
    return x


def conv_rows(padded, weight):
    height = padded.shape[0] - 2
    width = padded.shape[1]
    framed = jnp.pad(padded, ((0, 0), (1, 1), (0, 0)))
    patches = jnp.concatenate(
        [
            framed[row_off : row_off + height, col_off : col_off + width, :]
            for row_off in range(3)
            for col_off in range(3)
        ],
        axis=2,
    )
    inputs = weight.shape[2]
    result = jnp.dot(
        patches.reshape(height * width, 9 * inputs),
        weight.reshape(9 * inputs, weight.shape[3]),
        preferred_element_type=jnp.float32,
    )
    return result.reshape(height, width, weight.shape[3])


def lead_ahead(flat):
    rimmed = padded_2(flat.astype(jnp.bfloat16), (("span", 0),), 1).astype(flat.dtype)
    return rimmed[2:3]


def body(
    hidden_in,
    noisy_latents,
    span_ids,
    tile_map,
    qkv_weight,
    out_weight,
    norm_gain,
    velocity_weight,
    conv_first,
    conv_second,
):
    token_count = hidden_in.shape[0]
    inner = out_weight.shape[0]
    head_count = inner // HDIM
    devices = lax.axis_size("span")
    packed = jnp.dot(hidden_in, qkv_weight, preferred_element_type=jnp.float32).astype(jnp.bfloat16)
    query = jnp.maximum(packed[:, :inner], 0).reshape(token_count, head_count, HDIM)
    keys = jnp.maximum(packed[:, inner : 2 * inner], 0).reshape(token_count, head_count, HDIM)
    values = packed[:, 2 * inner :].reshape(token_count, head_count, HDIM)
    first_seg = span_ids[0]
    last_seg = span_ids[token_count - 1]
    last_value = last_seg.astype(jnp.float32)
    state = jnp.einsum("jhd,jhe->hde", keys, values, preferred_element_type=jnp.float32)
    key_sum = jnp.sum(keys, axis=0, dtype=jnp.float32)
    leading = (span_ids == first_seg).astype(jnp.bfloat16)
    lead_keys = keys * leading[:, None, None]
    lead_state = jnp.einsum("jhd,jhe->hde", lead_keys, values, preferred_element_type=jnp.float32)
    lead_sum = jnp.sum(lead_keys, axis=0, dtype=jnp.float32)
    first_value = first_seg.astype(jnp.float32).reshape(1)
    place = lax.axis_index("span")
    every_state, every_sum = (
        lax.all_gather(state[None].astype(jnp.bfloat16), "span", axis=0, tiled=True).astype(
            jnp.float32
        ),
        lax.all_gather(key_sum[None].astype(jnp.bfloat16), "span", axis=0, tiled=True).astype(
            jnp.float32
        ),
    )
    order = jnp.arange(every_state.shape[0], dtype=jnp.int32)
    below = (order < place).astype(jnp.float32)
    carry_state = jnp.sum(below[:, None, None, None] * every_state, axis=0)
    carry_sum = jnp.sum(below[:, None, None] * every_sum, axis=0)
    state_len = lead_state.size
    flat = jnp.concatenate([first_value, lead_state.reshape(-1), lead_sum.reshape(-1)])[None]
    next_one = lead_ahead(flat)
    next_two = lead_ahead(next_one)
    ahead = jnp.concatenate([next_one, next_two], axis=0)
    exists = place + jnp.arange(1, 3, dtype=jnp.int32) < devices
    match = (exists & (ahead[:, 0] == last_value)).astype(jnp.float32)
    picked = jnp.sum(match[:, None] * ahead[:, 1:], axis=0)
    after_state = picked[:state_len].reshape(lead_state.shape)
    after_sum = picked[state_len:].reshape(lead_sum.shape)
    query_f = query.astype(jnp.float32)
    tail_mask = (span_ids == last_seg).astype(jnp.float32)
    numer_carry = jnp.einsum("thd,hde->the", query_f, carry_state, precision=lax.Precision.HIGH)
    numer_carry = numer_carry + tail_mask[:, None, None] * jnp.einsum(
        "thd,hde->the", query_f, after_state, precision=lax.Precision.HIGH
    )
    denom_carry = jnp.einsum("thd,hd->th", query_f, carry_sum, precision=lax.Precision.HIGH)
    denom_carry = denom_carry + tail_mask[:, None] * jnp.einsum(
        "thd,hd->th", query_f, after_sum, precision=lax.Precision.HIGH
    )
    allowed = (span_ids[None, :] <= span_ids[:, None]).astype(jnp.float32)
    group = max([size_try for size_try in range(1, 8) if head_count % size_try == 0])
    passes = head_count // group

    def arrange(array):
        return jnp.transpose(array.reshape(token_count, passes, group, HDIM), (1, 2, 0, 3))

    def local_block(operands):
        query_b, keys_b, values_b = operands
        scores = (
            jnp.einsum("hid,hjd->hij", query_b, keys_b, preferred_element_type=jnp.float32)
            * allowed
        )
        numer = jnp.einsum(
            "hij,hje->hie", scores, values_b.astype(jnp.float32), precision=lax.Precision.HIGH
        )
        return (numer, jnp.sum(scores, axis=2))

    numer_local, denom_local = lax.map(
        local_block, (arrange(query), arrange(keys), arrange(values))
    )
    numer_local = jnp.transpose(numer_local.reshape(head_count, token_count, HDIM), (1, 0, 2))
    denom_local = jnp.transpose(denom_local.reshape(head_count, token_count), (1, 0))
    attention = (
        ((numer_local + numer_carry) / (1.0 + denom_local + denom_carry)[:, :, None])
        .reshape(token_count, inner)
        .astype(jnp.bfloat16)
    )
    mixed = hidden_in.astype(jnp.float32) + jnp.dot(
        attention, out_weight, preferred_element_type=jnp.float32
    )
    meansq = jnp.mean(mixed * mixed, axis=1, keepdims=True)
    normed = (mixed * lax.rsqrt(meansq + 1e-06) * norm_gain).astype(jnp.bfloat16)
    velocity = jnp.dot(normed, velocity_weight, preferred_element_type=jnp.float32)
    new_latents = noisy_latents - 0.5 * velocity
    share = token_count // devices
    mine_map = lax.dynamic_slice_in_dim(tile_map, place * token_count, token_count)
    target = mine_map // token_count
    hits = (target[:, None] == jnp.arange(devices, dtype=jnp.int32)[None, :]).astype(jnp.int32)
    rank = jnp.sum(jnp.cumsum(hits, axis=0) * hits, axis=1) - 1
    slot = target * share + rank
    outgoing = (
        jnp.zeros((devices * share, C), jnp.bfloat16)
        .at[slot]
        .set(new_latents.astype(jnp.bfloat16))
        .reshape(devices, share * C)
    )
    incoming = lax.all_to_all(outgoing, "span", split_axis=0, concat_axis=0, tiled=True)
    whole_map = tile_map.reshape(devices, token_count)
    arrive = whole_map // token_count == place
    order_in = jnp.cumsum(arrive.astype(jnp.int32), axis=1) - 1
    index = jnp.where(
        arrive, jnp.arange(devices, dtype=jnp.int32)[:, None] * share + order_in, devices * share
    )
    rows = (
        jnp.zeros((devices * share,), jnp.int32)
        .at[index.reshape(-1)]
        .set((whole_map % token_count).reshape(-1), mode="drop")
    )
    tile = (
        jnp.zeros((token_count, C), jnp.bfloat16)
        .at[rows]
        .set(incoming.reshape(devices * share, C))
        .reshape(token_count // IW, IW, C)
    )
    wide = padded_2(tile, (("span", 0),), 1)
    first = jax.nn.silu(conv_rows(wide, conv_first)).astype(jnp.bfloat16)
    first = padded_2(first, (("span", 0),), 1)
    decoded = conv_rows(first, conv_second).astype(jnp.bfloat16)
    return (new_latents, decoded)


def solution(mesh):
    placed = (
        P(("groups", "span"), None),
        P(("groups", "span"), None),
        P(("groups", "span")),
        P("groups"),
        P(),
        P(),
        P(),
        P(),
        P(),
        P(),
    )
    return jax.shard_map(
        body,
        mesh=mesh,
        in_specs=placed,
        out_specs=(P(("groups", "span"), None), P(("groups", "span"), None, None)),
        check_vma=False,
    )
```

profile of v0, /device:TPU:1, one launch (start us, length us, event | category | flops | bytes accessed | tf_op | source)
XLA Modules:
  0.0 191.3 jit_solution(17761613303931126227)
XLA Ops:
  8.6 19.7 %convolution_convert_fusion = bf16[512,3360]{0,1:T(8,128)(2,1)} fusion(bf16[512,2240]{0,1:T(8,128)(2,1)} %param.12, bf16[2240,3360]{1,0:T(8,128)(2,1)} %param.16), kind=kOutput, calls=%fused_computation.23 | convolution fusion | flops 7708753920 | bytes 20787200 | tf_op jit(solution)/shard_map/dot_general | solution.py:66
  29.6 2.7 %fusion.66 = (bf16[1120]{0:T(1024)(128)(2,1)S(1)}, bf16[1120]{0:T(1024)(128)(2,1)S(1)}, bf16[512,1120]{0,1:T(8,128)(2,1)S(1)}, bf16[512,1120]{0,1:T(8,128)(2,1)S(1)}, bf16[512,1120]{0,1:T(8,128)(2,1)S(1)}) fusion(bf16[512,3360]{0,1:T(8,128)(2,1)} %convolution_convert_fusion, bf16[512]{0:T(512)(128)(2,1)S(1)} %get-tuple-element.95), kind=kLoop, calls=%fused_computation.135 | loop fusion | flops 2864960 | bytes 6886784 | tf_op jit(solution)/shard_map/reduce_sum | solution.py:74
  35.2 2.4 %convolution_convert_fusion.1 = bf16[35,32,32]{2,1,0:T(8,128)(2,1)} fusion(bf16[512,35,32]{0,2,1:T(8,128)(2,1)S(1)} %bitcast.130, bf16[512,35,32]{0,2,1:T(8,128)(2,1)} %bitcast.133, bf16[512]{0:T(512)(128)(2,1)S(1)} %get-tuple-element.95), kind=kOutput, calls=%fused_computation.33 | convolution fusion | flops 37309440 | bytes 2366464 | tf_op jit(solution)/shard_map/jhd,jhe->hde/dot_general | solution.py:77
  37.6 1.8 concatenate.50
  40.6 3.7 %dynamic-update-slice.10 = bf16[1,36961]{1,0:T(2,128)(2,1)} dynamic-update-slice(bf16[1,36961]{1,0:T(2,128)(2,1)} %dynamic-update-slice.9, bf16[1,35840]{1,0:T(2,128)(2,1)} %concatenate.50, s32[]{} %constant.109, s32[]{} %constant.125) | dynamic-update-slice | bytes 143364
  45.8 1.9 %collective-permute-start = (bf16[1,36961]{1,0:T(2,128)(2,1)}, bf16[1,36961]{1,0:T(2,128)(2,1)}, u32[]{:S(2)}, u32[]{:S(2)}) collective-permute-start(bf16[1,36961]{1,0:T(2,128)(2,1)} %dynamic-update-slice.11), channel_id=1, source_target_pairs={{1,0},{2,1},{3,2},{4,3},{5,4},{6,5},{7,6},{8,7},{9,8},{10,9},{11,1... | collective-permute-start | bytes 221774 | tf_op jit(solution)/shard_map/ppermute | solution.py:19
  47.7 27.2 %while.13 = (s32[]{:T(128)}, f32[5,7,512,32]{2,3,1,0:T(8,128)}, f32[5,7,512]{2,1,0:T(8,128)}, bf16[5,7,512,32]{2,3,1,0:T(8,128)(2,1)S(1)}, bf16[5,7,512,32]{2,3,...) while((s32[]{:T(128)}, f32[5,7,512,32]{2,3,1,0:T(8,128)}, ...), condition=%wide.region_2.0_spmd.clone, body=%wide.region_0.2_spmd.clone.sunk | while | flops 475787776 | bytes 19021920 | solution.py:131
  47.9 2.1 %multiply_reduce_fusion.6 = (f32[7,512]{1,0:T(8,128)S(1)}, f32[7,512,512]{1,2,0:T(8,128)S(1)}) fusion(f32[512,512]{0,1:T(8,128)S(1)} %compare_convert_fusion.5, bf16[5,7,512,32]{2,3,1,0:T(8,128)(2,1)} %get-tuple-element.175, s32[]{:T(128)S(6)} %copy.74, bf16[5,7,512,32]{2,3,1,0:T(8,128)(2,1)S(1)} %get-tuple-element.174), kind=kOutput, calls=%fused_computation.4.clone.1 | convolution fusion | flops 121106944 | bytes 8862720 | tf_op jit(solution)/shard_map/while/body/eval_jaxpr/hid,hjd->hij/dot_general | solution.py:123
  50.0 2.5 %fusion.100 = f32[5,7,512,32]{2,3,1,0:T(8,128)} fusion(f32[5,7,512,32]{2,3,1,0:T(8,128)} %get-tuple-element.164, s32[]{:T(128)S(6)} %copy.74, f32[7,512,512]{1,2,0:T(8,128)S(1)} %get-tuple-element.153, f32[512,512]{0,1:T(8,128)S(1)} %compare_convert_fusion.5, bf16[5,7,512,32]{2,3,1,0:T(8,128)(2,1)S(1)} %get-tuple-element.176), kind=kOutput, calls=%fused_computation.9.clone.1 | convolution fusion | flops 354156544 | bytes 9077760 | tf_op jit(solution)/shard_map/while/body/eval_jaxpr/hij,hje->hie/dot_general | solution.py:126
  53.3 2.1 %multiply_reduce_fusion.6 = (f32[7,512]{1,0:T(8,128)S(1)}, f32[7,512,512]{1,2,0:T(8,128)S(1)}) fusion(f32[512,512]{0,1:T(8,128)S(1)} %compare_convert_fusion.5, bf16[5,7,512,32]{2,3,1,0:T(8,128)(2,1)} %get-tuple-element.175, s32[]{:T(128)S(6)} %copy.74, bf16[5,7,512,32]{2,3,1,0:T(8,128)(2,1)S(1)} %get-tuple-element.174), kind=kOutput, calls=%fused_computation.4.clone.1 | convolution fusion | flops 121106944 | bytes 8862720 | tf_op jit(solution)/shard_map/while/body/eval_jaxpr/hid,hjd->hij/dot_general | solution.py:123
  55.4 2.6 %fusion.100 = f32[5,7,512,32]{2,3,1,0:T(8,128)} fusion(f32[5,7,512,32]{2,3,1,0:T(8,128)} %get-tuple-element.164, s32[]{:T(128)S(6)} %copy.74, f32[7,512,512]{1,2,0:T(8,128)S(1)} %get-tuple-element.153, f32[512,512]{0,1:T(8,128)S(1)} %compare_convert_fusion.5, bf16[5,7,512,32]{2,3,1,0:T(8,128)(2,1)S(1)} %get-tuple-element.176), kind=kOutput, calls=%fused_computation.9.clone.1 | convolution fusion | flops 354156544 | bytes 9077760 | tf_op jit(solution)/shard_map/while/body/eval_jaxpr/hij,hje->hie/dot_general | solution.py:126
  58.7 2.1 %multiply_reduce_fusion.6 = (f32[7,512]{1,0:T(8,128)S(1)}, f32[7,512,512]{1,2,0:T(8,128)S(1)}) fusion(f32[512,512]{0,1:T(8,128)S(1)} %compare_convert_fusion.5, bf16[5,7,512,32]{2,3,1,0:T(8,128)(2,1)} %get-tuple-element.175, s32[]{:T(128)S(6)} %copy.74, bf16[5,7,512,32]{2,3,1,0:T(8,128)(2,1)S(1)} %get-tuple-element.174), kind=kOutput, calls=%fused_computation.4.clone.1 | convolution fusion | flops 121106944 | bytes 8862720 | tf_op jit(solution)/shard_map/while/body/eval_jaxpr/hid,hjd->hij/dot_general | solution.py:123
  60.9 2.6 %fusion.100 = f32[5,7,512,32]{2,3,1,0:T(8,128)} fusion(f32[5,7,512,32]{2,3,1,0:T(8,128)} %get-tuple-element.164, s32[]{:T(128)S(6)} %copy.74, f32[7,512,512]{1,2,0:T(8,128)S(1)} %get-tuple-element.153, f32[512,512]{0,1:T(8,128)S(1)} %compare_convert_fusion.5, bf16[5,7,512,32]{2,3,1,0:T(8,128)(2,1)S(1)} %get-tuple-element.176), kind=kOutput, calls=%fused_computation.9.clone.1 | convolution fusion | flops 354156544 | bytes 9077760 | tf_op jit(solution)/shard_map/while/body/eval_jaxpr/hij,hje->hie/dot_general | solution.py:126
  64.2 2.2 %multiply_reduce_fusion.6 = (f32[7,512]{1,0:T(8,128)S(1)}, f32[7,512,512]{1,2,0:T(8,128)S(1)}) fusion(f32[512,512]{0,1:T(8,128)S(1)} %compare_convert_fusion.5, bf16[5,7,512,32]{2,3,1,0:T(8,128)(2,1)} %get-tuple-element.175, s32[]{:T(128)S(6)} %copy.74, bf16[5,7,512,32]{2,3,1,0:T(8,128)(2,1)S(1)} %get-tuple-element.174), kind=kOutput, calls=%fused_computation.4.clone.1 | convolution fusion | flops 121106944 | bytes 8862720 | tf_op jit(solution)/shard_map/while/body/eval_jaxpr/hid,hjd->hij/dot_general | solution.py:123
  66.4 2.5 %fusion.100 = f32[5,7,512,32]{2,3,1,0:T(8,128)} fusion(f32[5,7,512,32]{2,3,1,0:T(8,128)} %get-tuple-element.164, s32[]{:T(128)S(6)} %copy.74, f32[7,512,512]{1,2,0:T(8,128)S(1)} %get-tuple-element.153, f32[512,512]{0,1:T(8,128)S(1)} %compare_convert_fusion.5, bf16[5,7,512,32]{2,3,1,0:T(8,128)(2,1)S(1)} %get-tuple-element.176), kind=kOutput, calls=%fused_computation.9.clone.1 | convolution fusion | flops 354156544 | bytes 9077760 | tf_op jit(solution)/shard_map/while/body/eval_jaxpr/hij,hje->hie/dot_general | solution.py:126
  69.7 2.1 %multiply_reduce_fusion.6 = (f32[7,512]{1,0:T(8,128)S(1)}, f32[7,512,512]{1,2,0:T(8,128)S(1)}) fusion(f32[512,512]{0,1:T(8,128)S(1)} %compare_convert_fusion.5, bf16[5,7,512,32]{2,3,1,0:T(8,128)(2,1)} %get-tuple-element.175, s32[]{:T(128)S(6)} %copy.74, bf16[5,7,512,32]{2,3,1,0:T(8,128)(2,1)S(1)} %get-tuple-element.174), kind=kOutput, calls=%fused_computation.4.clone.1 | convolution fusion | flops 121106944 | bytes 8862720 | tf_op jit(solution)/shard_map/while/body/eval_jaxpr/hid,hjd->hij/dot_general | solution.py:123
  71.8 2.5 %fusion.100 = f32[5,7,512,32]{2,3,1,0:T(8,128)} fusion(f32[5,7,512,32]{2,3,1,0:T(8,128)} %get-tuple-element.164, s32[]{:T(128)S(6)} %copy.74, f32[7,512,512]{1,2,0:T(8,128)S(1)} %get-tuple-element.153, f32[512,512]{0,1:T(8,128)S(1)} %compare_convert_fusion.5, bf16[5,7,512,32]{2,3,1,0:T(8,128)(2,1)S(1)} %get-tuple-element.176), kind=kOutput, calls=%fused_computation.9.clone.1 | convolution fusion | flops 354156544 | bytes 9077760 | tf_op jit(solution)/shard_map/while/body/eval_jaxpr/hij,hje->hie/dot_general | solution.py:126
  75.1 23.8 %all_gather.7 = bf16[16,35,32]{1,2,0:T(8,128)(2,1)S(1)} all-gather(bf16[1,35,32]{1,2,0:T(8,128)(2,1)S(1)} %copy.47), channel_id=1, replica_groups=mesh['groups'=2,'span'=16] {'span'}, dimensions={0}, use_global_device_ids=true | all-gather | bytes 38080 | tf_op jit(solution)/shard_map/all_gather | solution.py:85
  103.9 2.1 %collective-permute-start.1 = (bf16[1,36961]{1,0:T(2,128)(2,1)}, bf16[1,36961]{1,0:T(2,128)(2,1)S(1)}, u32[]{:S(2)}, u32[]{:S(2)}) collective-permute-start(bf16[1,36961]{1,0:T(2,128)(2,1)} %collective-permute-done), channel_id=1, source_target_pairs={{1,0},{2,1},{3,2},{4,3},{5,4},{6,5},{7,6},{8,7},{9,8},{10,9},{11,1... | collective-permute-start | bytes 221774 | tf_op jit(solution)/shard_map/ppermute | solution.py:19
  106.7 30.4 %scatter_custom_fusion = s32[512]{0:T(512)S(1)} fusion(s32[8192]{0:T(1024)S(1)} %get-tuple-element.93, s32[8192]{0:T(1024)S(1)} %get-tuple-element.92, s32[]{:T(128)} %constant.84.clone.1), kind=kCustom, calls=%fused_computation.132 | custom fusion | bytes 2052 | tf_op jit(solution)/shard_map/scatter | solution.py:170
  137.9 1.7 multiply_reduce_fusion.3
  140.4 3.8 %fusion.20 = f32[35,32,32]{2,1,0:T(8,128)S(1)} fusion(bf16[16,35,32,32]{3,2,1,0:T(8,128)(2,1)} %bitcast.135, f32[16]{0:T(128)S(1)} %compare_convert_fusion.3), kind=kLoop, calls=%fused_computation.22 | loop fusion | flops 1684480 | bytes 1290304 | tf_op jit(solution)/shard_map/reduce_sum | solution.py:91
  147.5 3.5 %multiply_reduce_fusion.1 = (f32[512]{0:T(512)S(1)}, f32[512,2240]{0,1:T(8,128)S(1)}) fusion(bf16[512,1120]{0,1:T(8,128)(2,1)S(1)} %bitcast.146, bf16[1120,2240]{1,0:T(8,128)(2,1)S(1)} %bitcast.144, bf16[512,2240]{0,1:T(8,128)(2,1)S(1)} %copy-done.7), kind=kOutput, calls=%fused_computation.26 | convolution fusion | flops 2573598208 | bytes 13047808 | tf_op jit(solution)/shard_map/dot_general | solution.py:141
  152.5 1.8 scatter_custom_fusion.1
  156.3 3.7 %all-to-all-start = ((bf16[16,2,512]{2,1,0:T(2,128)(2,1)}), bf16[16,2,512]{2,1,0:T(2,128)(2,1)S(1)}, u32[]{:S(2)}, u32[]{:S(2)}) async-start(bf16[16,2,512]{2,1,0:T(2,128)(2,1)} %reshape.279), calls=%async_computation | async-start | bytes 65536 | tf_op jit(solution)/shard_map/all_to_all | solution.py:160
  160.1 5.5 %all-to-all-done = bf16[16,2,512]{2,1,0:T(2,128)(2,1)S(1)} async-done(((bf16[16,2,512]{2,1,0:T(2,128)(2,1)}), bf16[16,2,512]{2,1,0:T(2,128)(2,1)S(1)}, u32[]{:S(2)}, u32[]{:S(2)}) %all-to-all-start) | async-done | bytes 32800 | tf_op jit(solution)/shard_map/all_to_all | solution.py:160
  166.0 1.8 scatter_custom_fusion.2
  167.8 2.7 %collective-permute-start.3 = (bf16[1,64,32]{2,1,0:T(8,128)(2,1)S(1)}, bf16[1,64,32]{2,1,0:T(8,128)(2,1)S(1)}, u32[]{:S(2)}, u32[]{:S(2)}) collective-permute-start(bf16[1,64,32]{2,1,0:T(8,128)(2,1)S(1)} %get-tuple-element.91), channel_id=1, source_target_pairs={{1,0},{2,1},{3,2},{4,3},{5,4},{6,5},{7,6},{8,7},{9,8},{10,9},{11,1... | collective-permute-start | bytes 12296 | tf_op jit(solution)/shard_map/ppermute | solution.py:19
  170.6 2.8 %collective-permute-start.2 = (bf16[1,64,32]{2,1,0:T(8,128)(2,1)S(1)}, bf16[1,64,32]{2,1,0:T(8,128)(2,1)S(1)}, u32[]{:S(2)}, u32[]{:S(2)}) collective-permute-start(bf16[1,64,32]{2,1,0:T(8,128)(2,1)S(1)} %get-tuple-element.90), channel_id=1, source_target_pairs={{0,1},{1,2},{2,3},{3,4},{4,5},{5,6},{6,7},{7,8},{8,9},{9,10},{10,1... | collective-permute-start | bytes 12296 | tf_op jit(solution)/shard_map/ppermute | solution.py:18
  175.3 1.9 %collective-permute-start.5 = (bf16[1,64,256]{2,1,0:T(8,128)(2,1)S(1)}, bf16[1,64,256]{2,1,0:T(8,128)(2,1)S(1)}, u32[]{:S(2)}, u32[]{:S(2)}) collective-permute-start(bf16[1,64,256]{2,1,0:T(8,128)(2,1)S(1)} %get-tuple-element.81), channel_id=1, source_target_pairs={{1,0},{2,1},{3,2},{4,3},{5,4},{6,5},{7,6},{8,7},{9,8},{10,9},{11,1... | collective-permute-start | bytes 98312 | tf_op jit(solution)/shard_map/ppermute | solution.py:19
  177.2 4.2 %collective-permute-start.4 = (bf16[1,64,256]{2,1,0:T(8,128)(2,1)S(1)}, bf16[1,64,256]{2,1,0:T(8,128)(2,1)S(1)}, u32[]{:S(2)}, u32[]{:S(2)}) collective-permute-start(bf16[1,64,256]{2,1,0:T(8,128)(2,1)S(1)} %get-tuple-element.80), channel_id=1, source_target_pairs={{0,1},{1,2},{2,3},{3,4},{4,5},{5,6},{6,7},{7,8},{8,9},{9,10},{10,1... | collective-permute-start | bytes 98312 | tf_op jit(solution)/shard_map/ppermute | solution.py:18
  182.9 1.5 convolution_convert_fusion.3
  (117 shorter events, 28.3 us)
Async XLA Ops:
  7.2 175.8 %copy-start = (bf16[3,3,256,256]{3,2,1,0:T(8,128)(2,1)S(1)}, bf16[3,3,256,256]{3,2,1,0:T(8,128)(2,1)}, u32[]{:S(2)}) copy-start(bf16[3,3,256,256]{3,2,1,0:T(8,128)(2,1)} %param.21) | copy-start | bytes 3538948
  7.2 133.2 %all-gather.3.cloned.1.call-start = ((), (), s32[]{:S(2)}) async-start(), calls=%async_computation.1 | async-start | bytes 4874240 | tf_op jit(solution)/shard_map/all_gather | solution.py:82
  8.6 19.7 %copy-start.2 = (s32[512]{0:T(512)S(1)}, s32[512]{0:T(512)}, u32[]{:S(2)}) copy-start(s32[512]{0:T(512)} %param.14) | copy-start | bytes 6148
  32.3 1.0 copy-start.1
  45.8 58.1 %collective-permute-start = (bf16[1,36961]{1,0:T(2,128)(2,1)}, bf16[1,36961]{1,0:T(2,128)(2,1)}, u32[]{:S(2)}, u32[]{:S(2)}) collective-permute-start(bf16[1,36961]{1,0:T(2,128)(2,1)} %dynamic-update-slice.11), channel_id=1, source_target_pairs={{1,0},{2,1},{3,2},{4,3},{5,4},{6,5},{7,6},{8,7},{9,8},{10,9},{11,1... | collective-permute-start | bytes 221774 | tf_op jit(solution)/shard_map/ppermute | solution.py:19
  47.7 51.3 %copy-start.3 = (s32[8192]{0:T(1024)S(1)}, s32[8192]{0:T(1024)}, u32[]{:S(2)}) copy-start(s32[8192]{0:T(1024)} %param.15) | copy-start | bytes 98308
  103.9 33.3 %collective-permute-start.1 = (bf16[1,36961]{1,0:T(2,128)(2,1)}, bf16[1,36961]{1,0:T(2,128)(2,1)S(1)}, u32[]{:S(2)}, u32[]{:S(2)}) collective-permute-start(bf16[1,36961]{1,0:T(2,128)(2,1)} %collective-permute-done), channel_id=1, source_target_pairs={{1,0},{2,1},{3,2},{4,3},{5,4},{6,5},{7,6},{8,7},{9,8},{10,9},{11,1... | collective-permute-start | bytes 221774 | tf_op jit(solution)/shard_map/ppermute | solution.py:19
  140.3 4.6 %copy-start.8 = (f32[5,7,512,32]{2,3,1,0:T(8,128)S(1)}, f32[5,7,512,32]{2,3,1,0:T(8,128)}, u32[]{:S(2)}) copy-start(f32[5,7,512,32]{2,3,1,0:T(8,128)} %get-tuple-element.40) | copy-start | bytes 6881284
  144.1 2.2 %slice-start = ((s8[5160960]{0:T(1024)(128)(4,1)}), s8[4194304]{0:T(1024)(128)(4,1)S(1)}, s32[]{:S(2)}) async-start(s8[5160960]{0:T(1024)(128)(4,1)} %bitcast.143), calls=%async_computation.2 | async-start | bytes 8388608
  145.0 2.5 %slice-start.1 = ((s8[5160960]{0:T(1024)(128)(4,1)}), s8[966656]{0:T(1024)(128)(4,1)S(1)}, s32[]{:S(2)}) async-start(s8[5160960]{0:T(1024)(128)(4,1)} %bitcast.143), calls=%async_computation.3 | async-start | bytes 1933312
  145.0 2.5 %copy-start.7 = (bf16[512,2240]{0,1:T(8,128)(2,1)S(1)}, bf16[512,2240]{0,1:T(8,128)(2,1)}, u32[]{:S(2)}) copy-start(bf16[512,2240]{0,1:T(8,128)(2,1)} %param.12) | copy-start | bytes 6881284
  147.5 3.5 %copy-start.4 = (bf16[2240,32]{0,1:T(8,128)(2,1)S(1)}, bf16[2240,32]{0,1:T(8,128)(2,1)}, u32[]{:S(2)}) copy-start(bf16[2240,32]{0,1:T(8,128)(2,1)} %param.19) | copy-start | bytes 430084
  147.5 3.5 %copy-start.5 = (f32[512,32]{0,1:T(8,128)S(1)}, f32[512,32]{0,1:T(8,128)}, u32[]{:S(2)}) copy-start(f32[512,32]{0,1:T(8,128)} %param.13) | copy-start | bytes 196612
  147.5 3.5 %copy-start.6 = (f32[2240]{0:T(1024)S(1)}, f32[2240]{0:T(1024)}, u32[]{:S(2)}) copy-start(f32[2240]{0:T(1024)} %param.18) | copy-start | bytes 26884
  156.3 18.6 %copy-start.9 = (bf16[3,3,32,256]{3,2,1,0:T(8,128)(2,1)S(1)}, bf16[3,3,32,256]{3,2,1,0:T(8,128)(2,1)}, u32[]{:S(2)}) copy-start(bf16[3,3,32,256]{3,2,1,0:T(8,128)(2,1)} %param.20) | copy-start | bytes 442372
  156.3 9.3 %all-to-all-start = ((bf16[16,2,512]{2,1,0:T(2,128)(2,1)}), bf16[16,2,512]{2,1,0:T(2,128)(2,1)S(1)}, u32[]{:S(2)}, u32[]{:S(2)}) async-start(bf16[16,2,512]{2,1,0:T(2,128)(2,1)} %reshape.279), calls=%async_computation | async-start | bytes 65536 | tf_op jit(solution)/shard_map/all_to_all | solution.py:160
  167.8 5.6 %collective-permute-start.3 = (bf16[1,64,32]{2,1,0:T(8,128)(2,1)S(1)}, bf16[1,64,32]{2,1,0:T(8,128)(2,1)S(1)}, u32[]{:S(2)}, u32[]{:S(2)}) collective-permute-start(bf16[1,64,32]{2,1,0:T(8,128)(2,1)S(1)} %get-tuple-element.91), channel_id=1, source_target_pairs={{1,0},{2,1},{3,2},{4,3},{5,4},{6,5},{7,6},{8,7},{9,8},{10,9},{11,1... | collective-permute-start | bytes 12296 | tf_op jit(solution)/shard_map/ppermute | solution.py:19
  170.6 3.7 %collective-permute-start.2 = (bf16[1,64,32]{2,1,0:T(8,128)(2,1)S(1)}, bf16[1,64,32]{2,1,0:T(8,128)(2,1)S(1)}, u32[]{:S(2)}, u32[]{:S(2)}) collective-permute-start(bf16[1,64,32]{2,1,0:T(8,128)(2,1)S(1)} %get-tuple-element.90), channel_id=1, source_target_pairs={{0,1},{1,2},{2,3},{3,4},{4,5},{5,6},{6,7},{7,8},{8,9},{9,10},{10,1... | collective-permute-start | bytes 12296 | tf_op jit(solution)/shard_map/ppermute | solution.py:18
  175.3 6.1 %collective-permute-start.5 = (bf16[1,64,256]{2,1,0:T(8,128)(2,1)S(1)}, bf16[1,64,256]{2,1,0:T(8,128)(2,1)S(1)}, u32[]{:S(2)}, u32[]{:S(2)}) collective-permute-start(bf16[1,64,256]{2,1,0:T(8,128)(2,1)S(1)} %get-tuple-element.81), channel_id=1, source_target_pairs={{1,0},{2,1},{3,2},{4,3},{5,4},{6,5},{7,6},{8,7},{9,8},{10,9},{11,1... | collective-permute-start | bytes 98312 | tf_op jit(solution)/shard_map/ppermute | solution.py:19
  177.2 5.2 %collective-permute-start.4 = (bf16[1,64,256]{2,1,0:T(8,128)(2,1)S(1)}, bf16[1,64,256]{2,1,0:T(8,128)(2,1)S(1)}, u32[]{:S(2)}, u32[]{:S(2)}) collective-permute-start(bf16[1,64,256]{2,1,0:T(8,128)(2,1)S(1)} %get-tuple-element.80), channel_id=1, source_target_pairs={{0,1},{1,2},{2,3},{3,4},{4,5},{5,6},{6,7},{7,8},{8,9},{9,10},{10,1... | collective-permute-start | bytes 98312 | tf_op jit(solution)/shard_map/ppermute | solution.py:18
Sparse Core Ops, SparseCore 0:
  34.6 55.8 all-gather.2
where the time goes:
time: 194 us; the launch traced here: 191 us
  matrix products  56.3 us (29%)
  local copies, waits for them, and re-layouts  52.3 us (27%)
  blocking collectives  23.8 us (12%)
  starting transfers between devices  19.5 us (10%)
  other arithmetic  16 us (8%)
  between operations  15.9 us (8%)
  waiting for transfers between devices  7.42 us (4%)
    scatter x1, local copies, waits for them, and re-layouts, body(): rows = jnp.zeros((devices * share,), jnp.int32).at[index.reshape(-1)].set...  30.4 us
    all_gather x1, blocking collectives, body(): lax.all_gather(key_sum[None].astype(jnp.bfloat16), 'span', axis=0, tiled=...  23.8 us
    dot_general x1, matrix products, body(): jnp.dot(hidden_in, qkv_weight, preferred_element_type=jnp.float32)  19.7 us
    dot_general x5, matrix products, local_block(): jnp.einsum('hij,hje->hie', scores, values_b.astype(jnp.float32), precisio...  12.8 us
    dot_general x5, matrix products, local_block(): jnp.einsum('hid,hjd->hij', query_b, keys_b, preferred_element_type=jnp.fl...  10.7 us
    ppermute x4, starting transfers between devices, padded_2(): after = lax.ppermute(first, axis, down)  8.64 us
    unnamed x36, local copies, waits for them, and re-layouts  8.12 us
    ppermute x2, starting transfers between devices, padded_2(): before = lax.ppermute(last, axis, up)  7.04 us
  transfers between devices with their start and end apart: 8, of which 3 were waited for; matrix products, arithmetic and copies ran while one was open for 40% of the time, Pallas kernels for 0%

commit v1 on v0

v1 whole, which is shorter than its diff:
```python
import functools

import jax
import jax.numpy as jnp
from jax import lax
from jax.experimental import pallas as pl
from jax.experimental.pallas import tpu as pltpu
from jax.sharding import PartitionSpec as P

HDIM = 32
IW = 64
BLK = 256
BF = jnp.bfloat16
F32 = jnp.float32


def dot(a, b):
    return jnp.dot(a, b, preferred_element_type=F32)


def dot_nt(a, b):
    return lax.dot_general(a, b, (((1,), (1,)), ((), ())), preferred_element_type=F32)


def dot_tn(a, b):
    return lax.dot_general(a, b, (((0,), (0,)), ((), ())), preferred_element_type=F32)


def iota(shape, axis):
    return lax.broadcasted_iota(jnp.int32, shape, axis)


def kernel(
    cfg,
    hid_hbm, noisy, span_ref, map_ref, wq_hbm, wo_hbm, gain, vw, w1, w2_hbm,
    lat_out, dec_out,
    hid, wq, wo, w2, packed, qs, ks, vs, num, kvis, att,
    st_c0, st_b0, st_send, lead_send, pair_recv, lead_recv, half_send, half_recv,
    fin_send, fin_recv, carry, after, onehot, posout, xlat, outgoing, incoming,
    wide, halo_send, halo_recv, first, shifted,
    wsem, lsem, psem, hsend, hrecv, fsem, lead_ssem, lead_rsem, asend, arecv, halo_ssem, halo_rsem,
):
    n, toks, d, inner, pad = cfg
    half = pad // 2
    chips = n // 2
    groups = pad // BLK
    me = lax.axis_index("span")
    core = lax.rem(me, 2)
    chip = me // 2
    partner = me + 1 - 2 * core
    share = toks // n
    chunk = toks // 2

    def remote(src, dst, ss, rs, dev):
        return pltpu.make_async_remote_copy(
            src_ref=src, dst_ref=dst, send_sem=ss, recv_sem=rs,
            device_id={"span": dev}, device_id_type=pl.DeviceIdType.MESH,
        )

    barrier = pltpu.get_barrier_semaphore()
    for k in range(1, n):
        pl.semaphore_signal(
            barrier, inc=1, device_id={"span": lax.rem(me + k, n)},
            device_id_type=pl.DeviceIdType.MESH,
        )

    total = wq_hbm.shape[1]
    full = total // BLK
    rest = total - full * BLK
    lo = inner // BLK

    def wcopy(b):
        cols = pl.ds(pl.multiple_of(b * BLK, BLK), BLK)
        return pltpu.make_async_copy(wq_hbm.at[:, cols], wq.at[:, cols], wsem.at[b])

    hcopy = pltpu.make_async_copy(hid_hbm, hid, lsem.at[0])
    hcopy.start()
    for b in range(lo, full):
        wcopy(b).start()
    tail_copy = None
    if rest:
        tail_copy = pltpu.make_async_copy(
            wq_hbm.at[:, full * BLK : total], wq.at[:, full * BLK : total], wsem.at[full]
        )
        tail_copy.start()
    for b in range(lo):
        wcopy(b).start()
    ocopy = pltpu.make_async_copy(wo_hbm, wo, lsem.at[1])
    ocopy.start()
    w2copy = pltpu.make_async_copy(w2_hbm, w2, lsem.at[2])
    w2copy.start()

    span_row = span_ref[...].astype(F32)
    span_col = jnp.transpose(jnp.broadcast_to(span_row, (128, toks)))[:, 0:1]
    first_seg = span_col[0:1, :]
    last_seg = span_col[toks - 1 : toks, :]
    lasts = [span_col[(c + 1) * chunk - 1 : (c + 1) * chunk, :] for c in range(2)]

    hcopy.wait()

    def project(b, carry_in):
        wcopy(b).wait()
        cols = pl.ds(pl.multiple_of(b * BLK, BLK), BLK)
        packed[:, cols] = dot(hid[...], wq[:, cols]).astype(BF)
        return carry_in

    lax.fori_loop(lo, full, project, 0)
    if rest:
        tail_copy.wait()
        packed[:, full * BLK : total] = dot(hid[...], wq[:, full * BLK : total]).astype(BF)

    def shift_in(dst, begin, relu):
        base = begin // 128 * 128
        off = begin - base
        width = packed.shape[1]
        end = min(base + pad + 128, width)

        def rows(r, c):
            rs = pl.ds(pl.multiple_of(r * 128, 128), 128)
            val = packed[rs, base:end].astype(F32)
            if off:
                val = pltpu.roll(val, val.shape[1] - off, 1)
            val = val[:, :pad]
            if relu:
                val = jnp.maximum(val, 0.0)
            val = jnp.where(iota((128, pad), 1) < inner, val, 0.0)
            dst[rs, :] = val.astype(BF)
            return c

        lax.fori_loop(0, toks // 128, rows, 0)

    shift_in(ks, inner, True)
    shift_in(vs, 2 * inner, False)

    block = (iota((BLK, BLK), 0) // HDIM == iota((BLK, BLK), 1) // HDIM)
    block_f = block.astype(F32)

    def compact(full_state):
        kept = jnp.where(block, full_state, 0.0)
        out = kept[0:HDIM]
        for h in range(1, BLK // HDIM):
            out = out + kept[h * HDIM : (h + 1) * HDIM]
        return out

    def expand(small):
        return (jnp.concatenate([small] * (BLK // HDIM), axis=0) * block_f).astype(BF)

    lead_col = (span_col == first_seg).astype(F32)
    to_b0 = (span_col[chunk:, :] <= lasts[0]).astype(F32)

    def states(g, c):
        cols = pl.ds(pl.multiple_of(g * BLK, BLK), BLK)
        k8 = ks[:, cols]
        v8 = vs[:, cols]
        s0 = compact(dot_tn(k8[:chunk], v8[:chunk]))
        s1 = compact(dot_tn(k8[chunk:], v8[chunk:]))
        k1 = (k8[chunk:].astype(F32) * to_b0).astype(BF)
        sb = compact(dot_tn(k1, v8[chunk:]))
        kl = (k8.astype(F32) * lead_col).astype(BF)
        sl = compact(dot_tn(kl, v8))
        st_c0[:, cols] = s0
        st_b0[:, cols] = s0 + sb
        num[0:HDIM, cols] = s0 + s1
        num[HDIM : 2 * HDIM, cols] = sl
        return c

    lax.fori_loop(0, groups, states, 0)

    def pack_sums(dst, column):
        kf = ks[...].astype(F32)
        if column is not None:
            kf = kf * column
        sums = jnp.sum(kf, axis=0, keepdims=True)
        parts = [sums[:, 128 * r : 128 * (r + 1)] for r in range((inner + 127) // 128)]
        base_rows = jnp.zeros((HDIM, 128), F32)
        row_no = iota((HDIM, 128), 0)
        for r, part in enumerate(parts):
            base_rows = jnp.where(row_no == r, jnp.broadcast_to(part, (HDIM, 128)), base_rows)
        base_rows = jnp.where(
            row_no == HDIM - 1, jnp.broadcast_to(first_seg, (HDIM, 128)), base_rows
        )
        dst[:, pad - 128 :] = base_rows.astype(BF)

    st_send[:, : pad - 128] = num[0:HDIM, : pad - 128].astype(BF)
    lead_send[:, : pad - 128] = num[HDIM : 2 * HDIM, : pad - 128].astype(BF)
    pack_sums(st_send, None)
    pack_sums(lead_send, lead_col)

    pl.semaphore_wait(barrier, n - 1)
    pair = remote(st_send, pair_recv, psem.at[0], psem.at[1], partner)
    pair.start()

    def lead_copy(k):
        return remote(
            lead_send, lead_recv.at[k], lead_ssem.at[k], lead_rsem.at[k],
            lax.rem(me - 1 - k + n, n),
        )

    for k in range(2):

        @pl.when(me >= k + 1)
        def _(k=k):
            lead_copy(k).start()

    mine = map_ref[pl.ds(me, 1), :]
    target = mine // toks
    within = mine - target * toks
    hits = (iota((n, toks), 0) == jnp.broadcast_to(target, (n, toks))).astype(F32)
    upper = (iota((toks, toks), 0) <= iota((toks, toks), 1)).astype(BF)
    cum = dot(hits.astype(BF), upper)
    rank = jnp.sum(cum * hits, axis=0, keepdims=True).astype(jnp.int32) - 1
    slot = target * share + rank
    onehot[...] = (iota((toks, toks), 0) == jnp.broadcast_to(slot, (toks, toks))).astype(F32).astype(BF)
    line = (within // IW).astype(F32)
    spot = (within - within // IW * IW).astype(F32)
    row_no = iota((128, toks), 0)
    places = jnp.where(row_no == HDIM, jnp.broadcast_to(spot, (128, toks)), 0.0)
    places = jnp.where(row_no == HDIM + 1, jnp.broadcast_to(line, (128, toks)), places)
    posout[...] = dot_nt(onehot[...], places.astype(BF))

    pair.wait()
    lanes = pl.ds(pl.multiple_of(core * half, 128), half)
    half_send[...] = (st_send[:, lanes].astype(F32) + pair_recv[:, lanes].astype(F32)).astype(BF)

    def chip_copy(to):
        return remote(
            half_send, half_recv.at[chip], hsend.at[to], hrecv.at[chip], 2 * to + core
        )

    for to in range(1, chips):

        @pl.when(chip < to)
        def _(to=to):
            chip_copy(to).start()

    lax.fori_loop(0, lo, project, 0)
    shift_in(qs, 0, True)

    heads_per = BLK // HDIM
    lane_head = iota((1, BLK), 1) // HDIM
    masks = []
    for c in range(2):
        sc = span_col[c * chunk : (c + 1) * chunk, :]
        sr = span_row[:, c * chunk : (c + 1) * chunk]
        keep = (sr <= sc) & (sc < lasts[c])
        masks.append(keep.astype(F32))
    allowed = (span_row <= span_col).astype(F32).astype(BF)

    def local(g, carry_in):
        cols = pl.ds(pl.multiple_of(g * BLK, BLK), BLK)
        kvis[:, cols] = dot(allowed, ks[:, cols])
        for c in range(2):
            rs = pl.ds(c * chunk, chunk)
            q8 = qs[rs, cols]
            k8 = ks[rs, cols]
            v8 = vs[rs, cols]
            acc = jnp.zeros((chunk, BLK), F32)
            for h in range(heads_per):
                hm = (lane_head == h).astype(F32).astype(BF)
                scores = (dot_nt(q8 * hm, k8) * masks[c]).astype(BF)
                acc = acc + dot(scores, v8 * hm)
            num[rs, cols] = acc
        return carry_in

    lax.fori_loop(0, groups, local, 0)

    fin_send[...] = jnp.zeros_like(fin_send)
    carry[:, lanes] = jnp.zeros((HDIM, half), F32)
    for src in range(chips - 1):

        @pl.when(src < chip)
        def _(src=src):
            remote(
                half_send, half_recv.at[src], hsend.at[src], hrecv.at[src], partner
            ).wait_recv()
            carry[:, lanes] = carry[:, lanes] + half_recv[src].astype(F32)

    fin_send[...] = carry[:, lanes].astype(BF)
    fin = remote(fin_send, fin_recv, fsem.at[0], fsem.at[1], partner)
    fin.start()
    after[...] = jnp.zeros_like(after)
    for k in range(2):

        @pl.when(me + 1 + k < n)
        def _(k=k):
            remote(
                lead_send, lead_recv.at[k], lead_ssem.at[k], lead_rsem.at[k], partner
            ).wait_recv()
            got = lead_recv[k].astype(F32)
            same = (got[HDIM - 1 : HDIM, pad - 128 : pad - 127] == last_seg).astype(F32)
            after[...] = after[...] + got * same

    fin.wait()
    other = pl.ds(pl.multiple_of((1 - core) * half, 128), half)
    carry[:, other] = fin_recv[...].astype(F32)

    @pl.when(core == 1)
    def _():
        carry[...] = carry[...] + pair_recv[...].astype(F32)

    reach = [(lasts[c] == last_seg).astype(F32) for c in range(2)]
    dev_tail = (span_col == last_seg).astype(F32)
    tails = [
        (span_col[c * chunk : (c + 1) * chunk, :] == lasts[c]).astype(F32) for c in range(2)
    ]
    ones_block = block_f.astype(BF)

    def spread(ref, g):
        per = BLK // 128
        rows = [ref[pl.ds(per * g + r, 1), pad - 128 :] for r in range(per)]
        return jnp.concatenate(rows, axis=1)

    for g in range(groups):
        cols = pl.ds(g * BLK, BLK)
        valid = iota((1, BLK), 1) + g * BLK < inner
        live = (iota((HDIM, BLK), 1) + g * BLK) < inner
        zero = jnp.zeros((HDIM, BLK), F32)
        car = jnp.where(live, carry[:, cols], zero)
        aft = jnp.where(live, after[:, cols], zero)
        if g * BLK + BLK <= (inner + 127) // 128 * 128:
            csum, asum = spread(carry, g), spread(after, g)
        else:
            need = (inner - g * BLK + 127) // 128
            csum = jnp.concatenate(
                [carry[2 * g + r : 2 * g + r + 1, pad - 128 :] if r < need
                 else jnp.zeros((1, 128), F32) for r in range(2)], axis=1)
            asum = jnp.concatenate(
                [after[2 * g + r : 2 * g + r + 1, pad - 128 :] if r < need
                 else jnp.zeros((1, 128), F32) for r in range(2)], axis=1)
        csum = jnp.where(valid, csum, 0.0)
        asum = jnp.where(valid, asum, 0.0)
        st_all = jnp.where(live, st_send[:, cols].astype(F32), zero)
        for c in range(2):
            rs = pl.ds(c * chunk, chunk)
            q8 = qs[rs, cols].astype(F32)
            q_tail = (q8 * tails[c]).astype(BF)
            q_non = (q8 * (1.0 - tails[c])).astype(BF)
            if c == 0:
                a_state = car
                b_state = st_b0[:, cols] + car + aft * reach[0]
            else:
                a_state = st_c0[:, cols] + car
                b_state = st_all + car + aft
            numer = num[rs, cols] + dot(q_non, expand(a_state)) + dot(q_tail, expand(b_state))
            seen = kvis[rs, cols] + csum + dev_tail[c * chunk : (c + 1) * chunk] * asum
            den = dot((q8 * seen).astype(BF), ones_block)
            att[rs, cols] = (numer / (1.0 + den)).astype(BF)

    ocopy.wait()
    xlat[...] = jnp.zeros_like(xlat)

    def tail_rows(r, c):
        rs = pl.ds(pl.multiple_of(r * BLK, BLK), BLK)
        mixed = hid[rs, :].astype(F32) + dot(att[rs, :inner], wo[...])
        meansq = jnp.sum(mixed * mixed, axis=1, keepdims=True) * (1.0 / d)
        normed = (mixed * lax.rsqrt(meansq + 1e-06) * gain[...]).astype(BF)
        lat = noisy[rs, :] - 0.5 * dot(normed, vw[...])
        lat_out[rs, :] = lat
        xlat[rs, 0:HDIM] = lat
        return c

    lax.fori_loop(0, toks // BLK, tail_rows, 0)

    outgoing[...] = (dot(onehot[...], xlat[...].astype(BF)) + posout[...]).astype(BF)

    def out_copy(k):
        to = lax.rem(me + k, n)
        return remote(
            outgoing.at[pl.ds(pl.multiple_of(to * share, share), share)],
            incoming.at[pl.ds(pl.multiple_of(me * share, share), share)],
            asend.at[k], arecv.at[me], to,
        )

    for k in range(1, n):
        out_copy(k).start()
    own = pl.ds(pl.multiple_of(me * share, share), share)
    incoming[own, :] = outgoing[own, :]
    for k in range(1, n):
        src = lax.rem(me + k, n)
        remote(
            outgoing.at[pl.ds(0, share)],
            incoming.at[pl.ds(pl.multiple_of(src * share, share), share)],
            asend.at[k], arecv.at[src], src,
        ).wait_recv()

    got = incoming[...]
    lane_no = iota((8, 128), 1)
    pick = jnp.where(lane_no == HDIM, 1.0, jnp.where(lane_no == HDIM + 1, float(IW), 0.0)).astype(BF)
    pos = dot_nt(pick, got)[0:1, :].astype(jnp.int32)
    onehot[...] = (iota((toks, toks), 0) == jnp.broadcast_to(pos, (toks, toks))).astype(F32).astype(BF)
    tile = dot(onehot[...], got)
    edge = 2 * IW
    wide[edge : edge + toks, :] = tile
    halo_send[0] = tile[:edge].astype(BF)
    halo_send[1] = tile[toks - edge :].astype(BF)

    def halo(k, to):
        return remote(halo_send.at[k], halo_recv.at[k], halo_ssem.at[k], halo_rsem.at[k], to)

    @pl.when(me > 0)
    def _():
        halo(0, me - 1).start()

    @pl.when(me < n - 1)
    def _():
        halo(1, me + 1).start()

    wide[0:edge, :] = jnp.zeros((edge, 128), F32)
    wide[edge + toks :, :] = jnp.zeros((edge, 128), F32)

    @pl.when(me > 0)
    def _():
        halo(1, partner).wait_recv()
        wide[0:edge, :] = halo_recv[1].astype(F32)

    @pl.when(me < n - 1)
    def _():
        halo(0, partner).wait_recv()
        wide[edge + toks :, :] = halo_recv[0].astype(F32)

    ext = toks + 2 * edge
    x = wide[...]
    column = lax.rem(iota((ext, 128), 0), IW)
    lane = iota((ext, 128), 1)
    left = jnp.where(column == 0, 0.0, pltpu.roll(x, 1, 0))
    right = jnp.where(column == IW - 1, 0.0, pltpu.roll(x, ext - 1, 0))
    three = jnp.where(
        lane < HDIM, left,
        jnp.where(lane < 2 * HDIM, pltpu.roll(x, HDIM, 1),
                  jnp.where(lane < 3 * HDIM, pltpu.roll(right, 2 * HDIM, 1), 0.0)),
    )
    three = three.astype(BF)
    mid = toks + 2 * IW
    k3 = 3 * HDIM
    acc = dot(three[0:mid, :k3], w1[0])
    acc = acc + dot(three[IW : IW + mid, :k3], w1[1])
    acc = acc + dot(three[2 * IW : 2 * IW + mid, :k3], w1[2])
    feat = acc / (1.0 + jnp.exp(-acc))
    row_at = iota((mid, 1), 0) // IW
    outside = ((row_at == 0) & (me == 0)) | ((row_at == mid // IW - 1) & (me == n - 1))
    feat = jnp.where(outside, 0.0, feat).astype(BF).astype(F32)
    column = lax.rem(iota((mid, 1), 0), IW)
    shifted[1] = feat.astype(BF)
    shifted[0] = jnp.where(column == 0, 0.0, pltpu.roll(feat, 1, 0)).astype(BF)
    shifted[2] = jnp.where(column == IW - 1, 0.0, pltpu.roll(feat, mid - 1, 0)).astype(BF)
    w2copy.wait()
    out = None
    for a in range(3):
        for b in range(3):
            part = dot(shifted[b, a * IW : a * IW + toks, :], w2[3 * a + b])
            out = part if out is None else out + part
    dec_out[...] = out.astype(BF)

    for k in range(2):

        @pl.when(me >= k + 1)
        def _(k=k):
            lead_copy(k).wait_send()

    for to in range(1, chips):

        @pl.when(chip < to)
        def _(to=to):
            chip_copy(to).wait_send()

    for k in range(1, n):
        out_copy(k).wait_send()

    @pl.when(me > 0)
    def _():
        halo(0, me - 1).wait_send()

    @pl.when(me < n - 1)
    def _():
        halo(1, me + 1).wait_send()


def body(
    hidden_in, noisy_latents, span_ids, tile_map, qkv_weight, out_weight,
    norm_gain, velocity_weight, conv_first, conv_second,
):
    toks, d = hidden_in.shape
    inner = out_weight.shape[0]
    n = lax.axis_size("span")
    pad = -(-(inner + 128) // BLK) * BLK
    ch = conv_first.shape[3]
    wide_cols = -(-qkv_weight.shape[1] // 128) * 128
    pack_cols = max(wide_cols, 2 * inner // 128 * 128 + pad + 128)
    chips = n // 2
    edge = 2 * IW
    mid = toks + 2 * IW
    blocks = -(-qkv_weight.shape[1] // BLK)
    vm, dma = pltpu.VMEM, pltpu.SemaphoreType.DMA
    any_, vmem = pl.BlockSpec(memory_space=pl.ANY), pl.BlockSpec(memory_space=pltpu.VMEM)
    scratch = [
        vm((toks, d), BF), vm(qkv_weight.shape, BF), vm(out_weight.shape, BF),
        vm((9, ch, ch), BF), vm((toks, pack_cols), BF),
        vm((toks, pad), BF), vm((toks, pad), BF), vm((toks, pad), BF),
        vm((toks, pad), F32), vm((toks, pad), F32), vm((toks, pad), BF),
        vm((HDIM, pad), F32), vm((HDIM, pad), F32),
        vm((HDIM, pad), BF), vm((HDIM, pad), BF), vm((HDIM, pad), BF), vm((2, HDIM, pad), BF),
        vm((HDIM, pad // 2), BF), vm((chips, HDIM, pad // 2), BF),
        vm((HDIM, pad // 2), BF), vm((HDIM, pad // 2), BF),
        vm((HDIM, pad), F32), vm((HDIM, pad), F32),
        vm((toks, toks), BF), vm((toks, 128), F32), vm((toks, 128), F32),
        vm((toks, 128), BF), vm((toks, 128), BF),
        vm((toks + 2 * edge, 128), F32), vm((2, edge, 128), BF), vm((2, edge, 128), BF),
        vm((8, 128), BF), vm((3, mid, ch), BF),
        dma((blocks,)), dma((3,)), dma((2,)), dma((chips,)), dma((chips,)), dma((2,)),
        dma((2,)), dma((2,)), dma((n,)), dma((n,)), dma((2,)), dma((2,)),
    ]
    latents, decoded = pl.pallas_call(
        functools.partial(kernel, (n, toks, d, inner, pad)),
        out_shape=(
            jax.ShapeDtypeStruct(noisy_latents.shape, F32),
            jax.ShapeDtypeStruct((toks, ch), BF),
        ),
        in_specs=[any_, vmem, vmem, vmem, any_, any_, vmem, vmem, vmem, any_],
        out_specs=(vmem, vmem),
        scratch_shapes=scratch,
        compiler_params=pltpu.CompilerParams(
            collective_id=0, has_side_effects=True, vmem_limit_bytes=60 * 1024 * 1024
        ),
    )(
        hidden_in, noisy_latents, span_ids.reshape(1, toks), tile_map.reshape(n, toks),
        qkv_weight, out_weight, norm_gain.reshape(1, d), velocity_weight,
        conv_first.reshape(3, 3 * HDIM, ch), conv_second.reshape(9, ch, ch),
    )
    return latents, decoded.reshape(toks // IW, IW, ch)


def solution(mesh):
    rows = P(("groups", "span"), None)
    placed = (rows, rows, P(("groups", "span")), P("groups")) + (P(),) * 6
    return jax.shard_map(
        body, mesh=mesh, in_specs=placed,
        out_specs=(rows, P(("groups", "span"), None, None)), check_vma=False,
    )
```

time: 194 us -> 69.9 us (0.36); the launches traced: 191 us -> 69.4 us
  matrix products: 56.3 us -> 0 us
  Pallas kernels: 0 us -> 54.8 us
  local copies, waits for them, and re-layouts: 52.3 us -> 14 us
  blocking collectives: 23.8 us -> 0 us
  starting transfers between devices: 19.5 us -> 0 us
  other arithmetic: 16 us -> 0 us
  between operations: 15.9 us -> 0.64 us
  waiting for transfers between devices: 7.42 us -> 0 us
    dot_general x21 -> x0, matrix products: 56.3 us -> none  [the longest x1 19.7 us: body(): jnp.dot(hidden_in, qkv_weight, preferred_element_type=jnp.float32)]
    pallas_call x0 -> x1, Pallas kernels: none -> 54.8 us  [body(): pl.pallas_call(functools.partial(kernel, (n, toks, d, inner, pad)), out_s...]
    scatter x3 -> x0, local copies, waits for them, and re-layouts: 34 us -> none  [the longest x1 30.4 us: body(): rows = jnp.zeros((devices * share,), jnp.int32).at[index.reshape(-1)].set...]
    all_gather x1 -> x0, blocking collectives: 23.8 us -> none  [body(): lax.all_gather(key_sum[None].astype(jnp.bfloat16), 'span', axis=0, tiled=...]
    ppermute x6 -> x0, starting transfers between devices: 15.7 us -> none  [the longest x4 8.64 us: padded_2(): after = lax.ppermute(first, axis, down)]
    reduce_sum x5 -> x0, other arithmetic: 8.31 us -> none  [the longest x1 3.78 us: body(): carry_state = jnp.sum(below[:, None, None, None] * every_state, axis=0)]
    all_to_all x1 -> x0, waiting for transfers between devices: 5.54 us -> none  [body(): lax.all_to_all(outgoing, 'span', split_axis=0, concat_axis=0, tiled=True)]
    concatenate x5 -> x0, local copies, waits for them, and re-layouts: 3.84 us -> none  [the longest x3 3.24 us: body(): jnp.concatenate([first_value, lead_state.reshape(-1), lead_sum.reshape(-1)])]
  transfers between devices with their start and end apart: 8 -> 0, of which waited for: 3 -> 0; matrix products, arithmetic and copies ran while one was open for 40% -> 0% of each run, Pallas kernels for 0% -> 0%
where the time goes in v1:
time: 69.9 us; the launch traced here: 69.4 us
  Pallas kernels  54.8 us (78%)
  local copies, waits for them, and re-layouts  14 us (20%)
    pallas_call x1, Pallas kernels, body(): pl.pallas_call(functools.partial(kernel, (n, toks, d, inner, pad)), out_s...  54.8 us
    unnamed x5, local copies, waits for them, and re-layouts  11.3 us

profile of v1, /device:TPU:1, one launch (start us, length us, event | category | flops | bytes accessed | tf_op | source)
XLA Modules:
  0.0 69.4 jit_solution(11992604699590613184)
XLA Ops:
  0.6 1.3 %reshape.24.gain = f32[1,2240]{1,0:T(1,128)} reshape(f32[2240]{0:T(1024)} %param.16) | data formatting | bytes 17920 | tf_op jit(solution)/shard_map/reshape | solution.py:526
  1.9 1.4 %reshape.23.map_ref = s32[16,512]{1,0:T(8,128)} reshape(s32[8192]{0:T(1024)} %param.13) | data formatting | bytes 65536 | tf_op jit(solution)/shard_map/reshape | solution.py:525
  3.3 1.7 %copy.13.noisy = f32[512,32]{1,0:T(8,128)} copy(f32[512,32]{0,1:T(8,128)} %param.11) | data formatting | bytes 131072 | tf_op args[1]
  5.0 2.0 %copy.14.vw = bf16[2240,32]{1,0:T(8,128)(2,1)} copy(bf16[2240,32]{0,1:T(8,128)(2,1)} %param.17) | data formatting | bytes 286720 | tf_op args[7]
  7.0 4.3 %copy.12.hid_hbm = bf16[512,2240]{1,0:T(8,128)(2,1)} copy(bf16[512,2240]{0,1:T(8,128)(2,1)} %param.10) | data formatting | bytes 4587520 | tf_op args[0]
  11.3 54.8 %shard_map.113 = (f32[512,32]{1,0:T(8,128)}, bf16[512,256]{1,0:T(8,128)(2,1)}) custom-call(bf16[512,2240]{1,0:T(8,128)(2,1)} %copy.12.hid_hbm, f32[512,32]{1,0:T(8,128)} %copy.13.noisy, s32[1,512]{1,0:T(1,128)} %bitcast.7, s32[16,512]{1,0:T(8,128)} %reshape.23.map_ref, bf16[2240,3360]{1,0:T(8,128)(2,1)} %wq_hbm.1, bf16[1120,2240]{1,0:T(8,128)(2,1)} %wo_hbm.1, ...), custom_call_target="tpu_custom_call" | custom-call | tf_op jit(solution)/shard_map/pallas_call | solution.py:512
  66.1 1.7 %copy.15 = f32[512,32]{0,1:T(8,128)} copy(f32[512,32]{1,0:T(8,128)} %get-tuple-element.6) | data formatting | bytes 131072
  67.8 1.7 %copy.17 = bf16[8,64,256]{2,1,0:T(8,128)(2,1)} copy(bf16[8,64,256]{2,1,0:T(8,128)(2,1)} %bitcast.5) | data formatting | bytes 524288

commit v2 on v1

--- a/solution.py
+++ b/solution.py
@@ -34,9 +34,9 @@
     cfg,
     hid_hbm, noisy, span_ref, map_ref, wq_hbm, wo_hbm, gain, vw, w1, w2_hbm,
     lat_out, dec_out,
-    hid, wq, wo, w2, packed, qs, ks, vs, num, kvis, att,
+    hidt, hid, wq, wo, w2, packed, qs, ks, vs, num, kvis, att,
     st_c0, st_b0, st_send, lead_send, pair_recv, lead_recv, half_send, half_recv,
-    fin_send, fin_recv, carry, after, onehot, posout, xlat, outgoing, incoming,
+    fin_send, fin_recv, carry, after, onehot, xlat, outgoing, incoming,
     wide, halo_send, halo_recv, first, shifted,
     wsem, lsem, psem, hsend, hrecv, fsem, lead_ssem, lead_rsem, asend, arecv, halo_ssem, halo_rsem,
 ):
@@ -73,7 +73,7 @@
         cols = pl.ds(pl.multiple_of(b * BLK, BLK), BLK)
         return pltpu.make_async_copy(wq_hbm.at[:, cols], wq.at[:, cols], wsem.at[b])
 
-    hcopy = pltpu.make_async_copy(hid_hbm, hid, lsem.at[0])
+    hcopy = pltpu.make_async_copy(hid_hbm, hidt, lsem.at[0])
     hcopy.start()
     for b in range(lo, full):
         wcopy(b).start()
@@ -97,6 +97,13 @@
     lasts = [span_col[(c + 1) * chunk - 1 : (c + 1) * chunk, :] for c in range(2)]
 
     hcopy.wait()
+
+    def turn(i, c):
+        cols = pl.ds(pl.multiple_of(i * 128, 128), 128)
+        hid[cols, :] = jnp.transpose(hidt[:, cols])
+        return c
+
+    lax.fori_loop(0, toks // 128, turn, 0)
 
     def project(b, carry_in):
         wcopy(b).wait()
@@ -202,7 +209,7 @@
         def _(k=k):
             lead_copy(k).start()
 
-    mine = map_ref[pl.ds(me, 1), :]
+    mine = map_ref[:, pl.ds(pl.multiple_of(me * toks, toks), toks)]
     target = mine // toks
     within = mine - target * toks
     hits = (iota((n, toks), 0) == jnp.broadcast_to(target, (n, toks))).astype(F32)
@@ -216,7 +223,7 @@
     row_no = iota((128, toks), 0)
     places = jnp.where(row_no == HDIM, jnp.broadcast_to(spot, (128, toks)), 0.0)
     places = jnp.where(row_no == HDIM + 1, jnp.broadcast_to(line, (128, toks)), places)
-    posout[...] = dot_nt(onehot[...], places.astype(BF))
+    xlat[...] = places
 
     pair.wait()
     lanes = pl.ds(pl.multiple_of(core * half, 128), half)
@@ -347,21 +354,20 @@
             att[rs, cols] = (numer / (1.0 + den)).astype(BF)
 
     ocopy.wait()
-    xlat[...] = jnp.zeros_like(xlat)
 
     def tail_rows(r, c):
         rs = pl.ds(pl.multiple_of(r * BLK, BLK), BLK)
         mixed = hid[rs, :].astype(F32) + dot(att[rs, :inner], wo[...])
         meansq = jnp.sum(mixed * mixed, axis=1, keepdims=True) * (1.0 / d)
-        normed = (mixed * lax.rsqrt(meansq + 1e-06) * gain[...]).astype(BF)
-        lat = noisy[rs, :] - 0.5 * dot(normed, vw[...])
-        lat_out[rs, :] = lat
-        xlat[rs, 0:HDIM] = lat
+        normed = (mixed * lax.rsqrt(meansq + 1e-06) * jnp.broadcast_to(gain[...][None, :], (BLK, d))).astype(BF)
+        lat = noisy[:, rs] - 0.5 * dot_nt(vw[...], normed)
+        lat_out[:, rs] = lat
+        xlat[0:HDIM, rs] = lat
         return c
 
     lax.fori_loop(0, toks // BLK, tail_rows, 0)
 
-    outgoing[...] = (dot(onehot[...], xlat[...].astype(BF)) + posout[...]).astype(BF)
+    outgoing[...] = dot_nt(onehot[...], xlat[...].astype(BF)).astype(BF)
 
     def out_copy(k):
         to = lax.rem(me + k, n)
@@ -493,7 +499,7 @@
     vm, dma = pltpu.VMEM, pltpu.SemaphoreType.DMA
     any_, vmem = pl.BlockSpec(memory_space=pl.ANY), pl.BlockSpec(memory_space=pltpu.VMEM)
     scratch = [
-        vm((toks, d), BF), vm(qkv_weight.shape, BF), vm(out_weight.shape, BF),
+        vm((d, toks), BF), vm((toks, d), BF), vm(qkv_weight.shape, BF), vm(out_weight.shape, BF),
         vm((9, ch, ch), BF), vm((toks, pack_cols), BF),
         vm((toks, pad), BF), vm((toks, pad), BF), vm((toks, pad), BF),
         vm((toks, pad), F32), vm((toks, pad), F32), vm((toks, pad), BF),
@@ -502,7 +508,7 @@
         vm((HDIM, pad // 2), BF), vm((chips, HDIM, pad // 2), BF),
         vm((HDIM, pad // 2), BF), vm((HDIM, pad // 2), BF),
         vm((HDIM, pad), F32), vm((HDIM, pad), F32),
-        vm((toks, toks), BF), vm((toks, 128), F32), vm((toks, 128), F32),
+        vm((toks, toks), BF), vm((128, toks), F32),
         vm((toks, 128), BF), vm((toks, 128), BF),
         vm((toks + 2 * edge, 128), F32), vm((2, edge, 128), BF), vm((2, edge, 128), BF),
         vm((8, 128), BF), vm((3, mid, ch), BF),
@@ -512,7 +518,7 @@
     latents, decoded = pl.pallas_call(
         functools.partial(kernel, (n, toks, d, inner, pad)),
         out_shape=(
-            jax.ShapeDtypeStruct(noisy_latents.shape, F32),
+            jax.ShapeDtypeStruct(noisy_latents.shape[::-1], F32),
             jax.ShapeDtypeStruct((toks, ch), BF),
         ),
         in_specs=[any_, vmem, vmem, vmem, any_, any_, vmem, vmem, vmem, any_],
@@ -522,11 +528,11 @@
             collective_id=0, has_side_effects=True, vmem_limit_bytes=60 * 1024 * 1024
         ),
     )(
-        hidden_in, noisy_latents, span_ids.reshape(1, toks), tile_map.reshape(n, toks),
-        qkv_weight, out_weight, norm_gain.reshape(1, d), velocity_weight,
+        hidden_in.T, noisy_latents.T, span_ids.reshape(1, toks), tile_map.reshape(1, -1),
+        qkv_weight, out_weight, norm_gain, velocity_weight.T,
         conv_first.reshape(3, 3 * HDIM, ch), conv_second.reshape(9, ch, ch),
     )
-    return latents, decoded.reshape(toks // IW, IW, ch)
+    return latents.T, decoded.reshape(toks // IW, IW, ch)
 
 
 def solution(mesh):

time: 69.9 us -> 59.5 us (0.85)
  local copies, waits for them, and re-layouts: 14 us -> 3.14 us
  Pallas kernels: 54.8 us -> 55.5 us
    unnamed x5 -> x2, local copies, waits for them, and re-layouts: 11.3 us -> 3.14 us
    reshape x2 -> x0, local copies, waits for them, and re-layouts: 2.68 us -> none  [the longest x1 1.38 us: body(): tile_map.reshape(n, toks)]
    pallas_call x1, Pallas kernels: 54.8 us -> 55.5 us  [body(): pl.pallas_call(functools.partial(kernel, (n, toks, d, inner, pad)), out_s...]
where the time goes in v2:
time: 59.5 us; the launch traced here: 59.3 us
  Pallas kernels  55.5 us (93%)
  local copies, waits for them, and re-layouts  3.14 us (5%)
  between operations  0.64 us (1%)
    pallas_call x1, Pallas kernels, body(): pl.pallas_call(functools.partial(kernel, (n, toks, d, inner, pad)), out_s...  55.5 us
    unnamed x2, local copies, waits for them, and re-layouts  3.14 us

profile of v2, /device:TPU:1, one launch (start us, length us, event | category | flops | bytes accessed | tf_op | source)
XLA Modules:
  0.0 59.3 jit_solution(3250037221286824733)
XLA Ops:
  0.6 55.5 %shard_map.113 = (f32[32,512]{1,0:T(8,128)}, bf16[512,256]{1,0:T(8,128)(2,1)}) custom-call(bf16[2240,512]{1,0:T(8,128)(2,1)} %bitcast.9, f32[32,512]{1,0:T(8,128)} %bitcast.14, s32[1,512]{1,0:T(1,128)} %bitcast.17, s32[1,8192]{1,0:T(1,128)} %bitcast.16, bf16[2240,3360]{1,0:T(8,128)(2,1)} %wq_hbm.1, bf16[1120,2240]{1,0:T(8,128)(2,1)} %wo_hbm.1, f32[2240]{0:T(1024)} %gain.1, ...), custom_call_target="tpu_custom_call" | custom-call | tf_op jit(solution)/shard_map/pallas_call | solution.py:518
  56.2 1.5 %copy.14 = f32[512,32]{0,1:T(8,128)} copy(f32[512,32]{0,1:T(8,128)} %bitcast.15) | data formatting | bytes 131072
  57.6 1.7 %copy.15 = bf16[8,64,256]{2,1,0:T(8,128)(2,1)} copy(bf16[8,64,256]{2,1,0:T(8,128)(2,1)} %bitcast.11) | data formatting | bytes 524288

commit v3 on v2

--- a/solution.py
+++ b/solution.py
@@ -253,23 +253,35 @@
         masks.append(keep.astype(F32))
     allowed = (span_row <= span_col).astype(F32).astype(BF)
 
-    def local(g, carry_in):
-        cols = pl.ds(pl.multiple_of(g * BLK, BLK), BLK)
+    def local(g, heads):
+        cols = pl.ds(g * BLK if isinstance(g, int) else pl.multiple_of(g * BLK, BLK), BLK)
         kvis[:, cols] = dot(allowed, ks[:, cols])
         for c in range(2):
             rs = pl.ds(c * chunk, chunk)
             q8 = qs[rs, cols]
             k8 = ks[rs, cols]
             v8 = vs[rs, cols]
-            acc = jnp.zeros((chunk, BLK), F32)
-            for h in range(heads_per):
-                hm = (lane_head == h).astype(F32).astype(BF)
-                scores = (dot_nt(q8 * hm, k8) * masks[c]).astype(BF)
-                acc = acc + dot(scores, v8 * hm)
+            acc = None
+            for h0 in range(0, heads, 2):
+                parts = []
+                vals = []
+                for h in range(h0, min(h0 + 2, heads)):
+                    hm = (lane_head == h).astype(F32).astype(BF)
+                    parts.append((dot_nt(q8 * hm, k8) * masks[c]).astype(BF))
+                    vals.append(v8 * hm)
+                one = dot(jnp.concatenate(parts, axis=1), jnp.concatenate(vals, axis=0))
+                acc = one if acc is None else acc + one
             num[rs, cols] = acc
+
+    whole = inner // BLK
+
+    def local_loop(g, carry_in):
+        local(g, heads_per)
         return carry_in
 
-    lax.fori_loop(0, groups, local, 0)
+    lax.fori_loop(0, whole, local_loop, 0)
+    if inner > whole * BLK:
+        local(whole, (inner - whole * BLK) // HDIM)
 
     fin_send[...] = jnp.zeros_like(fin_send)
     carry[:, lanes] = jnp.zeros((HDIM, half), F32)

time: 59.5 us -> 58.7 us (0.987)
  Pallas kernels: 55.5 us -> 54.7 us
    pallas_call x1, Pallas kernels: 55.5 us -> 54.7 us  [body(): pl.pallas_call(functools.partial(kernel, (n, toks, d, inner, pad)), out_s...]
where the time goes in v3:
time: 58.7 us; the launch traced here: 58.5 us
  Pallas kernels  54.7 us (93%)
  local copies, waits for them, and re-layouts  3.14 us (5%)
  between operations  0.64 us (1%)
    pallas_call x1, Pallas kernels, body(): pl.pallas_call(functools.partial(kernel, (n, toks, d, inner, pad)), out_s...  54.7 us
    unnamed x2, local copies, waits for them, and re-layouts  3.14 us

profile of v3, /device:TPU:1, one launch (start us, length us, event | category | flops | bytes accessed | tf_op | source)
XLA Modules:
  0.0 58.5 jit_solution(18385885964495303927)
XLA Ops:
  0.6 54.7 %shard_map.113 = (f32[32,512]{1,0:T(8,128)}, bf16[512,256]{1,0:T(8,128)(2,1)}) custom-call(bf16[2240,512]{1,0:T(8,128)(2,1)} %bitcast.9, f32[32,512]{1,0:T(8,128)} %bitcast.14, s32[1,512]{1,0:T(1,128)} %bitcast.17, s32[1,8192]{1,0:T(1,128)} %bitcast.16, bf16[2240,3360]{1,0:T(8,128)(2,1)} %wq_hbm.1, bf16[1120,2240]{1,0:T(8,128)(2,1)} %wo_hbm.1, f32[2240]{0:T(1024)} %gain.1, ...), custom_call_target="tpu_custom_call" | custom-call | tf_op jit(solution)/shard_map/pallas_call | solution.py:530
  55.4 1.5 %copy.14 = f32[512,32]{0,1:T(8,128)} copy(f32[512,32]{0,1:T(8,128)} %bitcast.15) | data formatting | bytes 131072
  56.8 1.7 %copy.15 = bf16[8,64,256]{2,1,0:T(8,128)(2,1)} copy(bf16[8,64,256]{2,1,0:T(8,128)(2,1)} %bitcast.11) | data formatting | bytes 524288
